TPU v7x, 32 devices: a whole 2x2x4 slice. The times are simulated.
32 devices in a mesh: frame: 4 (over y, x), row: 8 (over z, core).
Axes of the slice: x: 2, y: 2, z: 4, core: 2. Of those that a mesh axis runs over, the one named last changes fastest.
Arguments:
- residual_in: bfloat16 [4, 8, 64, 768], P('frame', 'row'), may hold values from -6 to 6
- q_spatial: bfloat16 [4, 8, 64, 768], P('frame', 'row'), may hold values from -250 to 250
- k_spatial: bfloat16 [4, 8, 64, 768], P('frame', 'row'), may hold values from -250 to 250
- v_spatial: bfloat16 [4, 8, 64, 768], P('frame', 'row'), may hold values from -6 to 6
- q_temporal: bfloat16 [4, 8, 64, 768], P('frame', 'row'), may hold values from -250 to 250
- k_temporal: bfloat16 [4, 8, 64, 768], P('frame', 'row'), may hold values from -250 to 250
- conv_weight: float32 [3, 3, 768], replicated, may hold values from -2 to 2
- conv_bias: float32 [768], replicated, may hold values from -3 to 3
Outputs:
- spatial_out: bfloat16 [4, 8, 64, 768], P('frame', 'row')
- block_out: bfloat16 [4, 8, 64, 768], P('frame', 'row')
All inputs are finite; a program needn't handle non-finite values.
Results may differ from a plain program's by a relative error of at most 0.0061.
Values may be sent and summed in bfloat16 or wider, within the bound.
A program may use at most 64 MiB of HBM per device.

v0:
```python
import functools
import math

import jax
import jax.numpy as jnp
from jax import lax
from jax.experimental import pallas as pl
from jax.experimental.pallas import tpu as pltpu
from jax.sharding import PartitionSpec as P

HEAD_DIM = 64
LANES = 2 * HEAD_DIM
SCALE = HEAD_DIM ** (-0.5)
LOG2E = math.log2(math.e)


def block_kernel(
    frames, rows, chunks, tokens, lent,
    res_hbm, q_hbm, k_hbm, v_hbm, qt_hbm, kt_hbm, cw_hbm, cb_hbm,
    so_hbm, bo_hbm,
    kv, qs, qh, oh, rs, qts, ktb, hb, tsc, wts, peak, rden, mixb, sob, bob, cwv, cbv,
    ld_kv, ld_misc, kv_recv, up_send, dn_send, pt_send,
    kt_recv, kt_send, h_recv, h_send, halo_recv, halo_send, out_sem, lend_sem, give_sem, back_sem,
):
    me_f = lax.axis_index("frame")
    me_r = lax.axis_index("row")
    chips = rows // 2
    z = me_r // 2
    core = me_r % 2
    at_end = jnp.logical_or(z == 0, z == chips - 1)
    helps = jnp.logical_or(z == 1, z == chips - 2)
    mate = me_r + 2 * jnp.where(jnp.logical_or(z == 0, z == chips - 2), 1, -1)

    def has_up(c):
        return z < chips - 1 - (1 if c < lent else 0)

    def has_down(c):
        return z > (1 if c < lent else 0)

    def attends(c):
        return jnp.logical_not(at_end) if c < lent else z >= 0

    def lanes(c):
        return pl.ds(c * LANES, LANES)

    for c in range(chunks):
        pltpu.make_async_copy(k_hbm.at[0, 0, :, lanes(c)], kv.at[me_r, c, 0], ld_kv.at[c]).start()
        pltpu.make_async_copy(v_hbm.at[0, 0, :, lanes(c)], kv.at[me_r, c, 1], ld_kv.at[c]).start()
    for c in range(chunks):
        pltpu.make_async_copy(kt_hbm.at[0, 0, :, lanes(c)], ktb.at[me_f, c], ld_misc.at[0]).start()
    for c in range(chunks):
        pltpu.make_async_copy(qt_hbm.at[0, 0, :, lanes(c)], qts.at[c], ld_misc.at[1]).start()
        pltpu.make_async_copy(q_hbm.at[0, 0, :, lanes(c)], qs.at[c], ld_misc.at[2]).start()
        pltpu.make_async_copy(res_hbm.at[0, 0, :, lanes(c)], rs.at[c], ld_misc.at[3]).start()
    pltpu.make_async_copy(cw_hbm, cwv, ld_misc.at[4]).start()
    pltpu.make_async_copy(cb_hbm, cbv, ld_misc.at[5]).start()

    barrier = pltpu.get_barrier_semaphore()

    def greet(**where):
        pl.semaphore_signal(
            barrier, inc=1, device_id=where, device_id_type=pl.DeviceIdType.MESH
        )

    greet(row=me_r + 1 - 2 * core)

    @pl.when(z > 0)
    def _():
        greet(row=me_r - 2)

    @pl.when(z < chips - 1)
    def _():
        greet(row=me_r + 2)

    across = me_r - 1 + 2 * core
    has_across = jnp.logical_and(across >= 0, across < rows)

    @pl.when(has_across)
    def _():
        greet(row=across)

    @pl.loop(1, frames)
    def _(step):
        greet(frame=(me_f + step) % frames)

    pl.semaphore_wait(
        barrier,
        frames
        + (z > 0).astype(jnp.int32)
        + (z < chips - 1).astype(jnp.int32)
        + has_across.astype(jnp.int32),
    )

    def remote(src, dst, send, recv, **where):
        return pltpu.make_async_remote_copy(
            src_ref=src, dst_ref=dst, send_sem=send, recv_sem=recv,
            device_id=where, device_id_type=pl.DeviceIdType.MESH,
        )

    def kv_copy(chip, of_core, c, send, to_row):
        src = 2 * chip + of_core
        return remote(kv.at[src, c], kv.at[src, c], send, kv_recv.at[src, c], row=to_row)

    def go_up(chip, c):
        return kv_copy(chip, core, c, up_send.at[chip], me_r + 2)

    def go_down(chip, c):
        return kv_copy(chip, core, c, dn_send.at[chip], me_r - 2)

    def to_partner(chip, c):
        return kv_copy(chip, core, c, pt_send.at[chip], me_r + 1 - 2 * core)

    def wait_slot(chip, of_core, c):
        kv_copy(chip, of_core, c, up_send.at[chip], me_r + 1 - 2 * core).wait_recv()

    def kt_copy(g, to):
        return remote(ktb.at[g], ktb.at[g], kt_send.at[to], kt_recv.at[g], frame=to)

    def h_copy(g, to, c):
        return remote(hb.at[g, c], hb.at[g, c], h_send.at[to], h_recv.at[g, c], frame=to)

    def halo_copy(side, c):
        return remote(
            mixb.at[1, c], mixb.at[2 - 2 * side, c], halo_send.at[side],
            halo_recv.at[1 - side, c], row=me_r - 1 + 2 * side,
        )

    def lend():
        return remote(qs.at[pl.ds(0, lent)], qh, lend_sem.at[0], lend_sem.at[1], row=mate)

    def give_back(c):
        return remote(oh.at[c], sob.at[c], give_sem.at[c], back_sem.at[c], row=mate)

    for c in range(chunks):
        pltpu.make_async_copy(kv.at[me_r, c], kv.at[me_r, c], ld_kv.at[c]).wait()

        @pl.when(has_down(c))
        def _(c=c):
            go_down(z, c).start()

        @pl.when(has_up(c))
        def _(c=c):
            go_up(z, c).start()

        @pl.when(attends(c))
        def _(c=c):
            to_partner(z, c).start()

    pltpu.make_async_copy(qs, qs, ld_misc.at[2]).wait()
    if lent:
        @pl.when(at_end)
        def _():
            lend().start()

    pltpu.make_async_copy(ktb.at[me_f], ktb.at[me_f], ld_misc.at[0]).wait()

    @pl.loop(me_f + 1, frames)
    def _(to):
        kt_copy(me_f, to).start()

    def relay(d, c):
        @pl.when(jnp.logical_and(z - d >= 0, attends(c)))
        def _():
            wait_slot(z - d, core, c)

            @pl.when(has_up(c))
            def _():
                go_up(z - d, c).start()

            to_partner(z - d, c).start()

        @pl.when(jnp.logical_and(z + d < chips, attends(c)))
        def _():
            wait_slot(z + d, core, c)

            @pl.when(has_down(c))
            def _():
                go_down(z + d, c).start()

            to_partner(z + d, c).start()

    last = jnp.maximum(z, chips - 1 - z)

    @pl.loop(1, last)
    def _(d):
        for c in range(chunks):
            relay(d, c)

    pltpu.make_async_copy(rs, rs, ld_misc.at[3]).wait()

    first_head = lax.broadcasted_iota(jnp.int32, (tokens, LANES), 1) < HEAD_DIM
    keys = rows * tokens

    def attend(blocks, c):
        none = jnp.zeros_like(blocks[0])
        queries = jnp.concatenate(
            [part for q in blocks
             for part in (jnp.where(first_head, q, none), jnp.where(first_head, none, q))],
            axis=0,
        )
        scores = lax.dot_general(
            queries, kv[:, c, 0].reshape(keys, LANES), (((1,), (1,)), ((), ())),
            preferred_element_type=jnp.float32,
        )
        top = jnp.max(scores, axis=1, keepdims=True)
        raised = jnp.exp2((scores - top) * (SCALE * LOG2E))
        denom = jnp.sum(raised, axis=1, keepdims=True)
        both = jnp.dot(
            raised.astype(jnp.bfloat16), kv[:, c, 1].reshape(keys, LANES),
            preferred_element_type=jnp.float32,
        ) / denom
        return [
            jnp.where(
                first_head,
                both[2 * i * tokens : (2 * i + 1) * tokens],
                both[(2 * i + 1) * tokens : (2 * i + 2) * tokens],
            ).astype(jnp.bfloat16)
            for i in range(len(blocks))
        ]

    for c in range(chunks):
        if c == 0:
            relay(last, 0)
        if c + 1 < chunks:
            relay(last, c + 1)

        @pl.when(attends(c))
        def _(c=c):
            @pl.loop(0, chips)
            def _(chip):
                wait_slot(chip, 1 - core, c)

        if c < lent:
            @pl.when(helps)
            def _(c=c):
                if c == 0:
                    lend().wait_recv()
                sob[c], oh[c] = attend([qs[c], qh[c]], c)
                give_back(c).start()

            @pl.when(at_end)
            def _(c=c):
                give_back(c).wait_recv()

            if chips > 4:
                @pl.when(jnp.logical_not(jnp.logical_or(at_end, helps)))
                def _(c=c):
                    sob[c] = attend([qs[c]], c)[0]
        else:
            sob[c] = attend([qs[c]], c)[0]

        hb[me_f, c] = (rs[c].astype(jnp.float32) + sob[c].astype(jnp.float32)).astype(jnp.bfloat16)

        @pl.loop(me_f + 1, frames)
        def _(to, c=c):
            h_copy(me_f, to, c).start()

        pltpu.make_async_copy(sob.at[c], so_hbm.at[0, 0, :, lanes(c)], out_sem.at[0]).start()

    pltpu.make_async_copy(qts, qts, ld_misc.at[1]).wait()

    @pl.loop(0, me_f)
    def _(g):
        kt_copy(g, me_f).wait_recv()

    flat = chunks * tokens
    same = (
        (lax.broadcasted_iota(jnp.int32, (2 * LANES, LANES), 0) // HEAD_DIM) % 2
        == lax.broadcasted_iota(jnp.int32, (2 * LANES, LANES), 1) // HEAD_DIM
    )
    spread = jnp.where(same, 1.0, 0.0).astype(jnp.bfloat16)
    peak[...] = jnp.full(peak.shape, -1e30, jnp.float32)

    @pl.loop(0, me_f + 1)
    def _(g):
        product = (
            qts[...].reshape(flat, LANES).astype(jnp.float32)
            * ktb[g].reshape(flat, LANES).astype(jnp.float32)
        )
        high = product.astype(jnp.bfloat16)
        low = (product - high.astype(jnp.float32)).astype(jnp.bfloat16)
        score = jnp.dot(
            jnp.concatenate([high, low], axis=1), spread, preferred_element_type=jnp.float32
        )
        tsc[g] = score
        peak[...] = jnp.maximum(peak[...], score)

    rden[...] = jnp.zeros(rden.shape, jnp.float32)

    @pl.loop(0, me_f + 1)
    def _(g):
        raised = jnp.exp2((tsc[g] - peak[...]) * (SCALE * LOG2E))
        rden[...] += raised
        wts[g] = raised.astype(jnp.bfloat16)

    rden[...] = 1.0 / rden[...]

    for c in range(chunks):
        @pl.loop(0, me_f)
        def _(g, c=c):
            h_copy(g, me_f, c).wait_recv()

        here = pl.ds(c * tokens, tokens)

        def add(g, total):
            return total + wts[g, here].astype(jnp.float32) * hb[g, c].astype(jnp.float32)

        total = lax.fori_loop(0, me_f + 1, add, jnp.zeros((tokens, LANES), jnp.float32))
        temporal = (total * rden[here]).astype(jnp.bfloat16)
        mixb[1, c] = (
            hb[me_f, c].astype(jnp.float32) + temporal.astype(jnp.float32)
        ).astype(jnp.bfloat16)

        @pl.when(me_r > 0)
        def _(c=c):
            halo_copy(0, c).start()

        @pl.when(me_r < rows - 1)
        def _(c=c):
            halo_copy(1, c).start()

    pltpu.make_async_copy(cwv, cwv, ld_misc.at[4]).wait()
    pltpu.make_async_copy(cbv, cbv, ld_misc.at[5]).wait()

    @pl.when(me_r == 0)
    def _():
        mixb[0] = jnp.zeros(mixb.shape[1:], mixb.dtype)

    @pl.when(me_r == rows - 1)
    def _():
        mixb[2] = jnp.zeros(mixb.shape[1:], mixb.dtype)

    position = lax.broadcasted_iota(jnp.int32, (tokens, LANES), 0)
    for c in range(chunks):
        @pl.when(me_r > 0)
        def _(c=c):
            remote(
                mixb.at[0, c], mixb.at[0, c], halo_send.at[0], halo_recv.at[0, c],
                row=me_r - 1,
            ).wait_recv()

        @pl.when(me_r < rows - 1)
        def _(c=c):
            remote(
                mixb.at[2, c], mixb.at[2, c], halo_send.at[1], halo_recv.at[1, c],
                row=me_r + 1,
            ).wait_recv()

        lines = [mixb[a, c].astype(jnp.float32) for a in range(3)]
        taps = [
            sum(cwv[a, pl.ds(b, 1), lanes(c)] * lines[a] for a in range(3)) for b in range(3)
        ]
        left = jnp.where(position == 0, 0.0, pltpu.roll(taps[0], 1, 0))
        right = jnp.where(position == tokens - 1, 0.0, pltpu.roll(taps[2], tokens - 1, 0))
        conv = cbv[pl.ds(c * LANES, LANES)].reshape(1, LANES) + taps[1] + left + right
        inner = math.sqrt(2.0 / math.pi) * (conv + 0.044715 * (conv * conv * conv))
        bob[c] = (lines[1] + 0.5 * conv * (1.0 + jnp.tanh(inner))).astype(jnp.bfloat16)
        pltpu.make_async_copy(bob.at[c], bo_hbm.at[0, 0, :, lanes(c)], out_sem.at[1]).start()

    def drain(ref, sem):
        pltpu.make_async_copy(ref, ref, sem).wait()

    some = pl.ds(lent, chunks - lent)

    @pl.loop(0, chips)
    def _(chip):
        src = 2 * chip + core

        @pl.when(at_end)
        def _():
            drain(kv.at[src, some], pt_send.at[chip])

        @pl.when(jnp.logical_not(at_end))
        def _():
            drain(kv.at[src], pt_send.at[chip])

    bound = 1 if lent else 0

    @pl.loop(0, z + 1)
    def _(chip):
        @pl.when(z < chips - 1 - bound)
        def _():
            drain(kv.at[2 * chip + core], up_send.at[chip])

        @pl.when(jnp.logical_and(z < chips - 1, z >= chips - 1 - bound))
        def _():
            drain(kv.at[2 * chip + core, some], up_send.at[chip])

    @pl.loop(z, chips)
    def _(chip):
        @pl.when(z > bound)
        def _():
            drain(kv.at[2 * chip + core], dn_send.at[chip])

        @pl.when(jnp.logical_and(z > 0, z <= bound))
        def _():
            drain(kv.at[2 * chip + core, some], dn_send.at[chip])

    @pl.loop(me_f + 1, frames)
    def _(to):
        kt_copy(me_f, to).wait_send()
        drain(hb.at[me_f], h_send.at[to])

    @pl.when(me_r > 0)
    def _():
        drain(mixb.at[1], halo_send.at[0])

    @pl.when(me_r < rows - 1)
    def _():
        drain(mixb.at[1], halo_send.at[1])

    if lent:
        @pl.when(at_end)
        def _():
            lend().wait_send()

    for c in range(lent):
        @pl.when(helps)
        def _(c=c):
            give_back(c).wait_send()

    pltpu.make_async_copy(sob, sob, out_sem.at[0]).wait()
    pltpu.make_async_copy(bob, bob, out_sem.at[1]).wait()


def on_device(frames, rows, *args):
    block = args[0]
    _, _, tokens, channels = block.shape
    chunks = channels // LANES
    chips = rows // 2
    lent = chunks * 3 // 6 if chips >= 4 else 0
    held = max(lent, 1)
    slab = (chunks, tokens, LANES)
    flat = (chunks * tokens, LANES)
    bf16, f32 = jnp.bfloat16, jnp.float32
    dma = pltpu.SemaphoreType.DMA
    anywhere = pl.BlockSpec(memory_space=pl.ANY)
    return pl.pallas_call(
        functools.partial(block_kernel, frames, rows, chunks, tokens, lent),
        out_shape=(jax.ShapeDtypeStruct(block.shape, bf16),) * 2,
        in_specs=[anywhere] * 8,
        out_specs=(anywhere, anywhere),
        scratch_shapes=[
            pltpu.VMEM((rows, chunks, 2, tokens, LANES), bf16),
            pltpu.VMEM(slab, bf16),
            pltpu.VMEM((held,) + slab[1:], bf16),
            pltpu.VMEM((held,) + slab[1:], bf16),
            pltpu.VMEM(slab, bf16),
            pltpu.VMEM(slab, bf16),
            pltpu.VMEM((frames,) + slab, bf16),
            pltpu.VMEM((frames,) + slab, bf16),
            pltpu.VMEM((frames,) + flat, f32),
            pltpu.VMEM((frames,) + flat, bf16),
            pltpu.VMEM(flat, f32),
            pltpu.VMEM(flat, f32),
            pltpu.VMEM((3,) + slab, bf16),
            pltpu.VMEM(slab, bf16),
            pltpu.VMEM(slab, bf16),
            pltpu.VMEM(args[6].shape, f32),
            pltpu.VMEM(args[7].shape, f32),
            dma((chunks,)), dma((6,)), dma((rows, chunks)),
            dma((chips,)), dma((chips,)), dma((chips,)),
            dma((frames,)), dma((frames,)), dma((frames, chunks)), dma((frames,)),
            dma((2, chunks)), dma((2,)), dma((2,)),
            dma((2,)), dma((held,)), dma((held,)),
        ],
        compiler_params=pltpu.CompilerParams(collective_id=0, has_side_effects=True,
            vmem_limit_bytes=(14 << 20) + (rows << 18) + (frames << 19)),
        name="block",
    )(*[pltpu.with_memory_space_constraint(a, pltpu.HBM) for a in args])


def solution(mesh):
    split = P("frame", "row", None, None)
    return jax.shard_map(
        functools.partial(on_device, mesh.shape["frame"], mesh.shape["row"]),
        mesh=mesh,
        in_specs=(split,) * 6 + (P(), P()),
        out_specs=(split, split),
        check_vma=False,
    )
```

profile of v0, /device:TPU:12, one launch (start us, length us, event | category | flops | bytes accessed | tf_op | source)
XLA Modules:
  0.0 27.0 jit_solution(313656160889678151)
XLA Ops:
  0.6 25.1 %block.1 = (bf16[1,1,64,768]{3,2,1,0:T(8,128)(2,1)S(1)}, bf16[1,1,64,768]{3,2,1,0:T(8,128)(2,1)S(1)}) custom-call(bf16[1,1,64,768]{3,2,1,0:T(8,128)(2,1)} %res_hbm.1, bf16[1,1,64,768]{3,2,1,0:T(8,128)(2,1)} %q_hbm.1, bf16[1,1,64,768]{3,2,1,0:T(8,128)(2,1)} %k_hbm.1, bf16[1,1,64,768]{3,2,1,0:T(8,128)(2,1)} %v_hbm.1, bf16[1,1,64,768]{3,2,1,0:T(8,128)(2,1)} %qt_hbm.1, ...), custom_call_target="tpu_custom_call" | custom-call | tf_op jit(solution)/shard_map/block/pallas_call | solution.py:438
  25.7 0.6 %copy.12 = bf16[1,1,64,768]{3,2,1,0:T(8,128)(2,1)} copy(bf16[1,1,64,768]{3,2,1,0:T(8,128)(2,1)S(1)} %get-tuple-element.4) | data formatting | bytes 196608
  26.4 0.6 %copy.13 = bf16[1,1,64,768]{3,2,1,0:T(8,128)(2,1)} copy(bf16[1,1,64,768]{3,2,1,0:T(8,128)(2,1)S(1)} %get-tuple-element.5) | data formatting | bytes 196608
where the time goes:
time: 27.2 us; the launch traced here: 27 us
  Pallas kernels  25.1 us (92%)
  local copies, waits for them, and re-layouts  1.28 us (5%)
  between operations  0.64 us (2%)
    pallas_call x1, Pallas kernels, on_device(): pl.pallas_call(functools.partial(block_kernel, frames, rows, chunks, toke...  25.1 us
    unnamed x2, local copies, waits for them, and re-layouts  1.28 us

commit v1 on v0

v1 whole, which is shorter than its diff:
```python
import functools
import math

import jax
import jax.numpy as jnp
from jax import lax
from jax.experimental import pallas as pl
from jax.experimental.pallas import tpu as pltpu
from jax.sharding import PartitionSpec as P

HEAD_DIM = 64
LANES = 2 * HEAD_DIM
SCALE = HEAD_DIM ** (-0.5)
LOG2E = math.log2(math.e)


def sent_tiles(rows, half, lent, z):
    chips = rows // 2
    at_end = z in (0, chips - 1)
    helps = z in (1, chips - 2)
    tiles = 2 * half
    for i in range(half):
        bound = 1 if i < lent else 0
        if z < chips - 1 - bound:
            tiles += 4 + 2 * 2 * z
        if z > bound:
            tiles += 4 + 2 * (rows - 2 * z - 2)
        if not (at_end and bound):
            tiles += 3
        if bound:
            tiles += 2 * (at_end + helps)
    return tiles


def block_kernel(
    frames, rows, chunks, tokens, lent,
    res_hbm, q_hbm, k_hbm, v_hbm, qt_hbm, kt_hbm, cw_hbm, cb_hbm,
    so_out, bo_out,
    kv, qs, ql, rs, rp, qts, ktb, hb, hp, sob, sop, sol, tsc, wts, peak, rden, mixb, cwv, cbv,
    void, hop, sent, ld, kv_recv, ql_recv, kt_recv, so_recv, h_recv, halo_recv,
):
    me_f = lax.axis_index("frame")
    me_r = lax.axis_index("row")
    half = chunks // 2
    chips = rows // 2
    z = me_r // 2
    core = me_r % 2
    pair = me_r + 1 - 2 * core
    at_end = jnp.logical_or(z == 0, z == chips - 1)
    helps = jnp.logical_or(z == 1, z == chips - 2)
    mate = z + jnp.where(jnp.logical_or(z == 0, z == chips - 2), 1, -1)
    bits = [1 << b for b in range((frames - 1).bit_length())]

    def bound(i):
        return 1 if i < lent else 0

    def has_up(i):
        return z < chips - 1 - bound(i)

    def has_down(i):
        return z > bound(i)

    def attends(i):
        return jnp.logical_not(at_end) if i < lent else z >= 0

    def lanes(c):
        if isinstance(c, int):
            return pl.ds(c * LANES, LANES)
        return pl.ds(pl.multiple_of(c * LANES, LANES), LANES)

    def mine(i):
        return core * half + i

    def other(i):
        return (1 - core) * half + i

    def cut(ref, c):
        return ref.at[0, 0, :, lanes(c)]

    def load(src, dst, sem):
        pltpu.make_async_copy(src, dst, sem).start()

    def drain(ref, sem):
        pltpu.make_async_copy(ref, ref, sem).wait()

    def take(tiles, sem):
        drain(void.at[pl.ds(0, tiles)], sem)

    def take_per_frame(tiles, sem):
        for g in range(frames):
            if tiles(g):
                @pl.when(me_f == g)
                def _(g=g):
                    take(tiles(g), sem)

    for i in range(half):
        @pl.when(attends(i))
        def _(i=i):
            load(cut(k_hbm, mine(i)), kv.at[me_r, i, 0], kv_recv.at[me_r, i])
            load(cut(v_hbm, mine(i)), kv.at[me_r, i, 1], kv_recv.at[me_r, i])
    for i in range(half):
        load(cut(q_hbm, mine(i)), qs.at[core, i], ld.at[0])
    for c in range(chunks):
        load(cut(kt_hbm, c), ktb.at[me_f, c], ld.at[1])
    for c in range(chunks):
        load(cut(qt_hbm, c), qts.at[c], ld.at[2])
        load(cut(res_hbm, c), rs.at[c], ld.at[0])
    load(cw_hbm, cwv, ld.at[3])
    load(cb_hbm, cbv, ld.at[4])

    def signal(sem, **where):
        pl.semaphore_signal(sem, inc=1, device_id=where, device_id_type=pl.DeviceIdType.MESH)

    def hear(sem, count):
        @pl.when(count > 0)
        def _():
            pl.semaphore_wait(sem, count)

    def over(b):
        return (me_f // b) % 2 == 0

    n_over = sum(over(b).astype(jnp.int32) for b in bits)
    n_under = len(bits) - n_over

    def tell_under(sem):
        for b in bits:
            @pl.when(jnp.logical_not(over(b)))
            def _(b=b):
                signal(sem, frame=me_f - b)

    barrier = pltpu.get_barrier_semaphore()
    signal(barrier, row=pair)

    @pl.when(z < chips - 1)
    def _():
        for k in range(2):
            signal(barrier, row=2 * (z + 1) + k)

    for b in bits:
        @pl.when(over(b))
        def _(b=b):
            signal(barrier, frame=me_f + b)

    pl.semaphore_wait(barrier, 1 + 2 * (z > 0).astype(jnp.int32) + n_under)

    @pl.when(z > 0)
    def _():
        for k in range(2):
            signal(hop.at[0], row=2 * (z - 1) + k)

    tell_under(hop.at[1])

    def remote(src, dst, send, recv, **where):
        return pltpu.make_async_remote_copy(
            src_ref=src, dst_ref=dst, send_sem=send, recv_sem=recv,
            device_id=where, device_id_type=pl.DeviceIdType.MESH,
        )

    def own_kv(i, p, row):
        for which, ref in enumerate((k_hbm, v_hbm)):
            remote(
                cut(ref, p * half + i), kv.at[me_r, i, which], sent.at[0], kv_recv.at[me_r, i], row=row
            ).start()

    def lend():
        for j in range(lent):
            for p in range(2):
                remote(
                    cut(q_hbm, p * half + j), ql.at[core, j], sent.at[0], ql_recv,
                    row=2 * mate + p,
                ).start()

    def kt_copy(g, to):
        return remote(ktb.at[g], ktb.at[g], sent.at[1], kt_recv, frame=to)

    for i in range(half):
        @pl.when(has_down(i))
        def _(i=i):
            for p in range(2):
                own_kv(i, p, 2 * (z - 1) + p)

        if i == 0 and lent:
            @pl.when(z == chips - 1)
            def _():
                lend()

    for i in range(half):
        @pl.when(attends(i))
        def _(i=i):
            own_kv(i, 1 - core, pair)

        remote(cut(q_hbm, other(i)), qs.at[core, i], sent.at[0], ld.at[0], row=pair).start()
        remote(cut(res_hbm, other(i)), rp.at[i], sent.at[0], ld.at[0], row=pair).start()

    @pl.when(z < chips - 1)
    def _():
        pl.semaphore_wait(hop.at[0], 2)

    for i in range(half):
        @pl.when(has_up(i))
        def _(i=i):
            for p in range(2):
                own_kv(i, p, 2 * (z + 1) + p)

        if i == 0 and lent:
            @pl.when(z == 0)
            def _():
                lend()

    drain(ktb.at[me_f], ld.at[1])
    depth = len(bits)
    hops = 2 + depth if depth < 3 else 3 * depth

    def above(m):
        return functools.reduce(jnp.logical_and, [over(b) for b in bits if m & b])

    def below(m):
        return functools.reduce(jnp.logical_and, [jnp.logical_not(over(b)) for b in bits if m & b])

    for level in range(depth):
        hear(hop.at[1 + level], n_over)
        if level + 1 < depth:
            tell_under(hop.at[2 + level])
        for m in range(1, frames):
            if bin(m).count("1") == level + 1:
                @pl.when(above(m))
                def _(m=m):
                    kt_copy(me_f, me_f + m).start()

    if depth > 2:
        for level in range(depth - 2):
            for b in bits:
                @pl.when(over(b))
                def _(b=b, level=level):
                    signal(hop.at[1 + depth + level], frame=me_f + b)

            hear(hop.at[1 + depth + level], n_under)
        for level in range(depth):
            tell_under(hop.at[2 * depth - 1 + level])
            hear(hop.at[2 * depth - 1 + level], n_over)

    for m in range(1, frames):
        for n in range(1, m):
            if m & n == 0:
                @pl.when(jnp.logical_and(above(m), below(n)))
                def _(m=m, n=n):
                    kt_copy(me_f, me_f + m - n).start()

    signal(hop.at[hops - 1], row=pair)

    def pass_kv(src, i, side):
        return remote(
            kv.at[src, i], kv.at[src, i], sent.at[0], kv_recv.at[src, i],
            row=me_r + 2 - 4 * side,
        )

    def relay(d, i):
        @pl.when(jnp.logical_and(z + d < chips, has_down(i)))
        def _():
            for k in range(2):
                src = 2 * (z + d) + k
                pass_kv(src, i, 1).wait_recv()
                pass_kv(src, i, 1).start()

        @pl.when(jnp.logical_and(z - d >= 0, has_up(i)))
        def _():
            for k in range(2):
                src = 2 * (z - d) + k
                pass_kv(src, i, 0).wait_recv()
                pass_kv(src, i, 0).start()

    last = jnp.maximum(z, chips - 1 - z)

    @pl.loop(1, jnp.where(at_end, 1, last))
    def _(d):
        for i in range(half):
            relay(d, i)

    def score_frames():
        drain(qts, ld.at[2])

        take_per_frame(lambda g: g * chunks, kt_recv)

        flat = chunks * tokens
        same = (
            (lax.broadcasted_iota(jnp.int32, (2 * LANES, LANES), 0) // HEAD_DIM) % 2
            == lax.broadcasted_iota(jnp.int32, (2 * LANES, LANES), 1) // HEAD_DIM
        )
        spread = jnp.where(same, 1.0, 0.0).astype(jnp.bfloat16)
        peak[...] = jnp.full(peak.shape, -1e30, jnp.float32)

        @pl.loop(0, me_f + 1)
        def _(g):
            product = (
                qts[...].reshape(flat, LANES).astype(jnp.float32)
                * ktb[g].reshape(flat, LANES).astype(jnp.float32)
            )
            high = product.astype(jnp.bfloat16)
            low = (product - high.astype(jnp.float32)).astype(jnp.bfloat16)
            score = jnp.dot(
                jnp.concatenate([high, low], axis=1), spread, preferred_element_type=jnp.float32
            )
            tsc[g] = score
            peak[...] = jnp.maximum(peak[...], score)

        rden[...] = jnp.zeros(rden.shape, jnp.float32)

        @pl.loop(0, me_f + 1)
        def _(g):
            raised = jnp.exp2((tsc[g] - peak[...]) * (SCALE * LOG2E))
            rden[...] += raised
            wts[g] = raised.astype(jnp.bfloat16)

        rden[...] = 1.0 / rden[...]

    @pl.when(at_end)
    def _():
        score_frames()

    pl.semaphore_wait(hop.at[hops - 1], 1)
    take(3 * half + chunks, ld.at[0])
    first_head = lax.broadcasted_iota(jnp.int32, (tokens, LANES), 1) < HEAD_DIM
    keys = rows * tokens

    def attend(blocks, i):
        none = jnp.zeros_like(blocks[0])
        queries = jnp.concatenate(
            [part for q in blocks
             for part in (jnp.where(first_head, q, none), jnp.where(first_head, none, q))],
            axis=0,
        )
        scores = lax.dot_general(
            queries, kv[:, i, 0].reshape(keys, LANES), (((1,), (1,)), ((), ())),
            preferred_element_type=jnp.float32,
        )
        top = jnp.max(scores, axis=1, keepdims=True)
        raised = jnp.exp2((scores - top) * (SCALE * LOG2E))
        denom = jnp.sum(raised, axis=1, keepdims=True)
        both = jnp.dot(
            raised.astype(jnp.bfloat16), kv[:, i, 1].reshape(keys, LANES),
            preferred_element_type=jnp.float32,
        ) / denom
        return [
            jnp.where(
                first_head,
                both[2 * b * tokens : (2 * b + 1) * tokens],
                both[(2 * b + 1) * tokens : (2 * b + 2) * tokens],
            ).astype(jnp.bfloat16)
            for b in range(len(blocks))
        ]

    def add(a, b):
        return (a.astype(jnp.float32) + b.astype(jnp.float32)).astype(jnp.bfloat16)

    def so_copy(i, c):
        return remote(sop.at[i], sob.at[c], sent.at[0], so_recv.at[i], row=pair)

    def sol_copy(i, k, c):
        return remote(sol.at[i, k], sob.at[c], sent.at[0], so_recv.at[i], row=2 * mate + k)

    def h_copy(src, to, row, i, c):
        return remote(
            src, hb.at[me_f, c], sent.at[1], h_recv.at[i], frame=to, row=row
        )

    def arrive(i):
        @pl.when(jnp.logical_not(at_end))
        def _():
            relay(last, i)

        @pl.when(attends(i))
        def _():
            drain(kv.at[me_r, i], kv_recv.at[me_r, i])
            remote(
                kv.at[pair, i], kv.at[pair, i], sent.at[0], kv_recv.at[pair, i], row=pair
            ).wait_recv()

            @pl.when(jnp.logical_not(has_up(i)))
            def _():
                @pl.loop(0, 2 * z)
                def _(src):
                    pass_kv(src, i, 1).wait_recv()

            @pl.when(jnp.logical_not(has_down(i)))
            def _():
                @pl.loop(2 * z + 2, rows)
                def _(src):
                    pass_kv(src, i, 0).wait_recv()

    def own(i):
        c = mine(i)
        sob[c], sop[i] = attend([qs[core, i], qs[1 - core, i]], i)
        so_copy(i, c).start()
        hb[me_f, c] = add(rs[c], sob[c])
        hp[i] = add(rp[i], sop[i])

        @pl.loop(me_f + 1, frames)
        def _(to):
            h_copy(hb.at[me_f, c], to, me_r, i, c).start()
            h_copy(hp.at[i], to, pair, i, c).start()

        so_out[0, 0, :, lanes(c)] = sob[c]

    def home(c):
        hb[me_f, c] = add(rs[c], sob[c])
        so_out[0, 0, :, lanes(c)] = sob[c]

    def settle_lent(i):
        take(2, so_recv.at[i])
        for p in range(2):
            c = p * half + i
            home(c)

            @pl.loop(me_f + 1, frames)
            def _(to, c=c):
                h_copy(hb.at[me_f, c], to, me_r, i, c).start()

    def settle(i):
        @pl.when(attends(i))
        def _():
            take(1, so_recv.at[i])
            home(other(i))

    def weigh(i):
        take_per_frame(lambda g: 2 * g, h_recv.at[i])
        for p in range(2):
            c = p * half + i
            here = pl.ds(c * tokens, tokens)

            def step(g, total, c=c, here=here):
                return total + wts[g, here].astype(jnp.float32) * hb[g, c].astype(jnp.float32)

            total = lax.fori_loop(0, me_f + 1, step, jnp.zeros((tokens, LANES), jnp.float32))
            temporal = (total * rden[here]).astype(jnp.bfloat16)
            mixb[1, c] = add(hb[me_f, c], temporal)

            @pl.when(me_r > 0)
            def _(c=c):
                halo_copy(0, i, c).start()

            @pl.when(me_r < rows - 1)
            def _(c=c):
                halo_copy(1, i, c).start()

    def halo_copy(side, i, c):
        return remote(
            mixb.at[1, c], mixb.at[2 - 2 * side, c], sent.at[2], halo_recv.at[i], row=me_r - 1 + 2 * side
        )

    edges = (me_r > 0).astype(jnp.int32) + (me_r < rows - 1).astype(jnp.int32)
    position = lax.broadcasted_iota(jnp.int32, (tokens, LANES), 0)

    def convolve(i):
        for sides in (1, 2):
            @pl.when(edges == sides)
            def _(sides=sides):
                take(2 * sides, halo_recv.at[i])

        for p in range(2):
            c = p * half + i
            lines = [mixb[a, c].astype(jnp.float32) for a in range(3)]
            taps = [
                sum(cwv[a, pl.ds(b, 1), lanes(c)] * lines[a] for a in range(3)) for b in range(3)
            ]
            left = jnp.where(position == 0, 0.0, pltpu.roll(taps[0], 1, 0))
            right = jnp.where(position == tokens - 1, 0.0, pltpu.roll(taps[2], tokens - 1, 0))
            conv = cbv[pl.ds(c * LANES, LANES)].reshape(1, LANES) + taps[1] + left + right
            inner = math.sqrt(2.0 / math.pi) * (conv + 0.044715 * (conv * conv * conv))
            bo_out[0, 0, :, lanes(c)] = (
                lines[1] + 0.5 * conv * (1.0 + jnp.tanh(inner))
            ).astype(jnp.bfloat16)

    @pl.when(me_r == 0)
    def _():
        mixb[0] = jnp.zeros(mixb.shape[1:], mixb.dtype)

    @pl.when(me_r == rows - 1)
    def _():
        mixb[2] = jnp.zeros(mixb.shape[1:], mixb.dtype)

    if lent:
        @pl.when(at_end)
        def _():
            for i in range(lent):
                settle_lent(i)

    for i in range(half):
        arrive(i)
        if i < lent:
            @pl.when(helps)
            def _(i=i):
                if i == 0:
                    drain(ql, ql_recv)
                sol[i, 0], sol[i, 1] = attend([ql[0, i], ql[1, i]], i)
                for k in range(2):
                    sol_copy(i, k, mine(i)).start()

            @pl.when(jnp.logical_not(at_end))
            def _(i=i):
                own(i)
        else:
            own(i)

    @pl.when(jnp.logical_not(at_end))
    def _():
        score_frames()

    drain(cwv, ld.at[3])
    drain(cbv, ld.at[4])
    for i in range(half):
        settle(i)
        weigh(i)
    for i in range(half):
        convolve(i)
    for s in range(chips):
        @pl.when(z == s)
        def _(s=s):
            take(sent_tiles(rows, half, lent, s), sent.at[0])

    take_per_frame(lambda g: (frames - 1 - g) * 2 * chunks, sent.at[1])
    for sides in (1, 2):
        @pl.when(edges == sides)
        def _(sides=sides):
            take(sides * chunks, sent.at[2])


def store_kernel(so, bo, so_hbm, bo_hbm, sem):
    copies = [
        pltpu.make_async_copy(so, so_hbm, sem.at[0]),
        pltpu.make_async_copy(bo, bo_hbm, sem.at[1]),
    ]
    for copy in copies:
        copy.start()
    for copy in copies:
        copy.wait()


def on_device(frames, rows, *args):
    block = args[0]
    _, _, tokens, channels = block.shape
    chunks = channels // LANES
    half = chunks // 2
    chips = rows // 2
    lent = 1 if chips >= 4 else 0
    held = max(lent, 1)
    tile = (tokens, LANES)
    slab = (chunks,) + tile
    flat = (chunks * tokens, LANES)
    bf16, f32 = jnp.bfloat16, jnp.float32
    dma = pltpu.SemaphoreType.DMA
    anywhere = pl.BlockSpec(memory_space=pl.ANY)
    vmem = pl.BlockSpec(memory_space=pltpu.VMEM)
    outs = (jax.ShapeDtypeStruct(block.shape, bf16),) * 2
    room = max(
        [sent_tiles(rows, half, lent, s) for s in range(chips)] + [frames * 2 * chunks]
    )
    levels = (frames - 1).bit_length()
    mixed = pl.pallas_call(
        functools.partial(block_kernel, frames, rows, chunks, tokens, lent),
        out_shape=outs,
        in_specs=[anywhere] * 8,
        out_specs=(vmem, vmem),
        scratch_shapes=[
            pltpu.VMEM((rows, half, 2) + tile, bf16),
            pltpu.VMEM((2, half) + tile, bf16),
            pltpu.VMEM((2, held) + tile, bf16),
            pltpu.VMEM(slab, bf16),
            pltpu.VMEM((half,) + tile, bf16),
            pltpu.VMEM(slab, bf16),
            pltpu.VMEM((frames,) + slab, bf16),
            pltpu.VMEM((frames,) + slab, bf16),
            pltpu.VMEM((half,) + tile, bf16),
            pltpu.VMEM(slab, bf16),
            pltpu.VMEM((half,) + tile, bf16),
            pltpu.VMEM((held, 2) + tile, bf16),
            pltpu.VMEM((frames,) + flat, f32),
            pltpu.VMEM((frames,) + flat, bf16),
            pltpu.VMEM(flat, f32),
            pltpu.VMEM(flat, f32),
            pltpu.VMEM((3,) + slab, bf16),
            pltpu.VMEM(args[6].shape, f32),
            pltpu.VMEM(args[7].shape, f32),
            pltpu.VMEM((room,) + tile, bf16),
            pltpu.SemaphoreType.REGULAR((2 + levels if levels < 3 else 3 * levels,)),
            dma((3,)), dma((5,)), dma((rows, half)), dma, dma, dma((half,)), dma((half,)), dma((half,)),
        ],
        compiler_params=pltpu.CompilerParams(collective_id=0, has_side_effects=True,
            vmem_limit_bytes=(14 << 20) + (rows << 18) + (frames << 19)),
        name="block",
    )(*[pltpu.with_memory_space_constraint(a, pltpu.HBM) for a in args])
    return pl.pallas_call(
        store_kernel,
        out_shape=outs,
        in_specs=[vmem, vmem],
        out_specs=(anywhere, anywhere),
        scratch_shapes=[dma((2,))],
        compiler_params=pltpu.CompilerParams(vmem_limit_bytes=4 << 20),
        name="store",
    )(*mixed)


def solution(mesh):
    split = P("frame", "row", None, None)
    return jax.shard_map(
        functools.partial(on_device, mesh.shape["frame"], mesh.shape["row"]),
        mesh=mesh,
        in_specs=(split,) * 6 + (P(), P()),
        out_specs=(split, split),
        check_vma=False,
    )
```

time: 27.2 us -> 24.5 us (0.901)
  the two profiles are of different devices: /device:TPU:12 before, /device:TPU:21 now
where the time goes in v1:
time: 24.5 us; the launch traced here: 24.4 us
  Pallas kernels  23.8 us (97%)
  between operations  0.64 us (3%)
    pallas_call x1, Pallas kernels, on_device(): pl.pallas_call(functools.partial(block_kernel, frames, rows, chunks, toke...  23.1 us
    pallas_call x1, Pallas kernels, on_device(): pl.pallas_call(store_kernel, out_shape=outs, in_specs=[vmem, vmem], out_s...  0.69 us

profile of v1, /device:TPU:21, one launch (start us, length us, event | category | flops | bytes accessed | tf_op | source)
XLA Modules:
  0.0 24.4 jit_solution(7956158236510689053)
XLA Ops:
  0.6 23.1 %block.1 = (bf16[1,1,64,768]{3,2,1,0:T(8,128)(2,1)S(1)}, bf16[1,1,64,768]{3,2,1,0:T(8,128)(2,1)S(1)}) custom-call(bf16[1,1,64,768]{3,2,1,0:T(8,128)(2,1)} %res_hbm.1, bf16[1,1,64,768]{3,2,1,0:T(8,128)(2,1)} %q_hbm.1, bf16[1,1,64,768]{3,2,1,0:T(8,128)(2,1)} %k_hbm.1, bf16[1,1,64,768]{3,2,1,0:T(8,128)(2,1)} %v_hbm.1, bf16[1,1,64,768]{3,2,1,0:T(8,128)(2,1)} %qt_hbm.1, ...), custom_call_target="tpu_custom_call" | custom-call | tf_op jit(solution)/shard_map/block/pallas_call | solution.py:558
  23.7 0.7 %store.1 = (bf16[1,1,64,768]{3,2,1,0:T(8,128)(2,1)}, bf16[1,1,64,768]{3,2,1,0:T(8,128)(2,1)}) custom-call(bf16[1,1,64,768]{3,2,1,0:T(8,128)(2,1)S(1)} %get-tuple-element.4.so, bf16[1,1,64,768]{3,2,1,0:T(8,128)(2,1)S(1)} %get-tuple-element.5.bo), custom_call_target="tpu_custom_call" | custom-call | tf_op jit(solution)/shard_map/store/pallas_call | solution.py:591

commit v2 on v1

--- a/solution.py
+++ b/solution.py
@@ -20,7 +20,7 @@
     helps = z in (1, chips - 2)
     tiles = 2 * half
     for i in range(half):
-        bound = 1 if i < lent else 0
+        bound = 1 if i >= half - lent else 0
         if z < chips - 1 - bound:
             tiles += 4 + 2 * 2 * z
         if z > bound:
@@ -28,7 +28,7 @@
         if not (at_end and bound):
             tiles += 3
         if bound:
-            tiles += 2 * (at_end + helps)
+            tiles += 4 * at_end + 2 * helps
     return tiles
 
 
@@ -36,7 +36,7 @@
     frames, rows, chunks, tokens, lent,
     res_hbm, q_hbm, k_hbm, v_hbm, qt_hbm, kt_hbm, cw_hbm, cb_hbm,
     so_out, bo_out,
-    kv, qs, ql, rs, rp, qts, ktb, hb, hp, sob, sop, sol, tsc, wts, peak, rden, mixb, cwv, cbv,
+    kv, qs, ql, rl, rs, rp, qts, ktb, hb, hp, sob, sop, sol, hl, tsc, wts, peak, rden, mixb, cwv, cbv,
     void, hop, sent, ld, kv_recv, ql_recv, kt_recv, so_recv, h_recv, halo_recv,
 ):
     me_f = lax.axis_index("frame")
@@ -52,7 +52,7 @@
     bits = [1 << b for b in range((frames - 1).bit_length())]
 
     def bound(i):
-        return 1 if i < lent else 0
+        return 1 if i >= half - lent else 0
 
     def has_up(i):
         return z < chips - 1 - bound(i)
@@ -61,7 +61,7 @@
         return z > bound(i)
 
     def attends(i):
-        return jnp.logical_not(at_end) if i < lent else z >= 0
+        return jnp.logical_not(at_end) if bound(i) else z >= 0
 
     def lanes(c):
         if isinstance(c, int):
@@ -93,6 +93,89 @@
                 def _(g=g):
                     take(tiles(g), sem)
 
+    def signal(sem, **where):
+        pl.semaphore_signal(sem, inc=1, device_id=where, device_id_type=pl.DeviceIdType.MESH)
+
+    def hear(sem, count):
+        @pl.when(count > 0)
+        def _():
+            pl.semaphore_wait(sem, count)
+
+    def over(b):
+        return (me_f // b) % 2 == 0
+
+    n_over = sum(over(b).astype(jnp.int32) for b in bits)
+    n_under = len(bits) - n_over
+
+    def tell_under(sem):
+        for b in bits:
+            @pl.when(jnp.logical_not(over(b)))
+            def _(b=b):
+                signal(sem, frame=me_f - b)
+
+    barrier = pltpu.get_barrier_semaphore()
+    signal(barrier, row=pair)
+
+    @pl.when(z < chips - 1)
+    def _():
+        for k in range(2):
+            signal(barrier, row=2 * (z + 1) + k)
+
+    for b in bits:
+        @pl.when(over(b))
+        def _(b=b):
+            signal(barrier, frame=me_f + b)
+
+    pl.semaphore_wait(barrier, 1 + 2 * (z > 0).astype(jnp.int32) + n_under)
+
+    @pl.when(z > 0)
+    def _():
+        for k in range(2):
+            signal(hop.at[0], row=2 * (z - 1) + k)
+
+    tell_under(hop.at[1])
+
+    def remote(src, dst, send, recv, **where):
+        return pltpu.make_async_remote_copy(
+            src_ref=src, dst_ref=dst, send_sem=send, recv_sem=recv,
+            device_id=where, device_id_type=pl.DeviceIdType.MESH,
+        )
+
+    def own_kv(i, p, row):
+        for which, ref in enumerate((k_hbm, v_hbm)):
+            remote(
+                cut(ref, p * half + i), kv.at[me_r, i, which], sent.at[0], kv_recv.at[me_r, i], row=row
+            ).start()
+
+    def lend():
+        for j in range(lent):
+            for p in range(2):
+                c = p * half + half - lent + j
+                for src, dst in ((q_hbm, ql), (res_hbm, rl)):
+                    remote(
+                        cut(src, c), dst.at[core, j], sent.at[0], ql_recv, row=2 * mate + p
+                    ).start()
+
+    def kt_copy(g, to):
+        return remote(ktb.at[g], ktb.at[g], sent.at[1], kt_recv, frame=to)
+
+    for i in range(half):
+        @pl.when(has_down(i))
+        def _(i=i):
+            for p in range(2):
+                own_kv(i, p, 2 * (z - 1) + p)
+
+    for i in range(half):
+        @pl.when(attends(i))
+        def _(i=i):
+            own_kv(i, 1 - core, pair)
+
+        remote(cut(q_hbm, other(i)), qs.at[core, i], sent.at[0], ld.at[0], row=pair).start()
+        remote(cut(res_hbm, other(i)), rp.at[i], sent.at[0], ld.at[0], row=pair).start()
+
+    for c in range(chunks):
+        load(cut(kt_hbm, c), ktb.at[me_f, c], ld.at[1])
+
     for i in range(half):
         @pl.when(attends(i))
         def _(i=i):
@@ -100,98 +183,12 @@
             load(cut(v_hbm, mine(i)), kv.at[me_r, i, 1], kv_recv.at[me_r, i])
     for i in range(half):
         load(cut(q_hbm, mine(i)), qs.at[core, i], ld.at[0])
-    for c in range(chunks):
-        load(cut(kt_hbm, c), ktb.at[me_f, c], ld.at[1])
     for c in range(chunks):
         load(cut(qt_hbm, c), qts.at[c], ld.at[2])
         load(cut(res_hbm, c), rs.at[c], ld.at[0])
     load(cw_hbm, cwv, ld.at[3])
     load(cb_hbm, cbv, ld.at[4])
 
-    def signal(sem, **where):
-        pl.semaphore_signal(sem, inc=1, device_id=where, device_id_type=pl.DeviceIdType.MESH)
-
-    def hear(sem, count):
-        @pl.when(count > 0)
-        def _():
-            pl.semaphore_wait(sem, count)
-
-    def over(b):
-        return (me_f // b) % 2 == 0
-
-    n_over = sum(over(b).astype(jnp.int32) for b in bits)
-    n_under = len(bits) - n_over
-
-    def tell_under(sem):
-        for b in bits:
-            @pl.when(jnp.logical_not(over(b)))
-            def _(b=b):
-                signal(sem, frame=me_f - b)
-
-    barrier = pltpu.get_barrier_semaphore()
-    signal(barrier, row=pair)
-
-    @pl.when(z < chips - 1)
-    def _():
-        for k in range(2):
-            signal(barrier, row=2 * (z + 1) + k)
-
-    for b in bits:
-        @pl.when(over(b))
-        def _(b=b):
-            signal(barrier, frame=me_f + b)
-
-    pl.semaphore_wait(barrier, 1 + 2 * (z > 0).astype(jnp.int32) + n_under)
-
-    @pl.when(z > 0)
-    def _():
-        for k in range(2):
-            signal(hop.at[0], row=2 * (z - 1) + k)
-
-    tell_under(hop.at[1])
-
-    def remote(src, dst, send, recv, **where):
-        return pltpu.make_async_remote_copy(
-            src_ref=src, dst_ref=dst, send_sem=send, recv_sem=recv,
-            device_id=where, device_id_type=pl.DeviceIdType.MESH,
-        )
-
-    def own_kv(i, p, row):
-        for which, ref in enumerate((k_hbm, v_hbm)):
-            remote(
-                cut(ref, p * half + i), kv.at[me_r, i, which], sent.at[0], kv_recv.at[me_r, i], row=row
-            ).start()
-
-    def lend():
-        for j in range(lent):
-            for p in range(2):
-                remote(
-                    cut(q_hbm, p * half + j), ql.at[core, j], sent.at[0], ql_recv,
-                    row=2 * mate + p,
-                ).start()
-
-    def kt_copy(g, to):
-        return remote(ktb.at[g], ktb.at[g], sent.at[1], kt_recv, frame=to)
-
-    for i in range(half):
-        @pl.when(has_down(i))
-        def _(i=i):
-            for p in range(2):
-                own_kv(i, p, 2 * (z - 1) + p)
-
-        if i == 0 and lent:
-            @pl.when(z == chips - 1)
-            def _():
-                lend()
-
-    for i in range(half):
-        @pl.when(attends(i))
-        def _(i=i):
-            own_kv(i, 1 - core, pair)
-
-        remote(cut(q_hbm, other(i)), qs.at[core, i], sent.at[0], ld.at[0], row=pair).start()
-        remote(cut(res_hbm, other(i)), rp.at[i], sent.at[0], ld.at[0], row=pair).start()
-
     @pl.when(z < chips - 1)
     def _():
         pl.semaphore_wait(hop.at[0], 2)
@@ -202,10 +199,10 @@
             for p in range(2):
                 own_kv(i, p, 2 * (z + 1) + p)
 
-        if i == 0 and lent:
-            @pl.when(z == 0)
-            def _():
-                lend()
+    if lent:
+        @pl.when(at_end)
+        def _():
+            lend()
 
     drain(ktb.at[me_f], ld.at[1])
     depth = len(bits)
@@ -247,6 +244,11 @@
                     kt_copy(me_f, me_f + m - n).start()
 
     signal(hop.at[hops - 1], row=pair)
+    if lent:
+        @pl.when(at_end)
+        def _():
+            for p in range(2):
+                signal(hop.at[hops - 1], row=2 * mate + p)
 
     def pass_kv(src, i, side):
         return remote(
@@ -317,7 +319,7 @@
     def _():
         score_frames()
 
-    pl.semaphore_wait(hop.at[hops - 1], 1)
+    pl.semaphore_wait(hop.at[hops - 1], 1 + 2 * helps.astype(jnp.int32) if lent else 1)
     take(3 * half + chunks, ld.at[0])
     first_head = lax.broadcasted_iota(jnp.int32, (tokens, LANES), 1) < HEAD_DIM
     keys = rows * tokens
@@ -352,11 +354,25 @@
     def add(a, b):
         return (a.astype(jnp.float32) + b.astype(jnp.float32)).astype(jnp.bfloat16)
 
+    def each_later(send):
+        if frames > 4:
+            @pl.loop(me_f + 1, frames)
+            def _(to):
+                send(to)
+            return
+        ways = [(m, n) for m in range(1, frames) for n in range(m) if m & n == 0]
+        for m, n in sorted(ways, key=lambda way: -bin(way[0] | way[1]).count("1")):
+            @pl.when(jnp.logical_and(above(m), below(n)) if n else above(m))
+            def _(m=m, n=n):
+                send(me_f + m - n)
+
     def so_copy(i, c):
         return remote(sop.at[i], sob.at[c], sent.at[0], so_recv.at[i], row=pair)
 
     def sol_copy(i, k, c):
-        return remote(sol.at[i, k], sob.at[c], sent.at[0], so_recv.at[i], row=2 * mate + k)
+        return remote(
+            sol.at[i - half + lent, k], sob.at[c], sent.at[0], so_recv.at[i], row=2 * mate + k
+        )
 
     def h_copy(src, to, row, i, c):
         return remote(
@@ -390,32 +406,29 @@
     def own(i):
         c = mine(i)
         sob[c], sop[i] = attend([qs[core, i], qs[1 - core, i]], i)
-        so_copy(i, c).start()
         hb[me_f, c] = add(rs[c], sob[c])
         hp[i] = add(rp[i], sop[i])
 
-        @pl.loop(me_f + 1, frames)
-        def _(to):
+        def send(to):
             h_copy(hb.at[me_f, c], to, me_r, i, c).start()
             h_copy(hp.at[i], to, pair, i, c).start()
 
+        each_later(send)
+        so_copy(i, c).start()
         so_out[0, 0, :, lanes(c)] = sob[c]
 
     def home(c):
         hb[me_f, c] = add(rs[c], sob[c])
         so_out[0, 0, :, lanes(c)] = sob[c]
 
-    def settle_lent(i):
-        take(2, so_recv.at[i])
-        for p in range(2):
-            c = p * half + i
-            home(c)
-
-            @pl.loop(me_f + 1, frames)
-            def _(to, c=c):
-                h_copy(hb.at[me_f, c], to, me_r, i, c).start()
-
     def settle(i):
+        if bound(i):
+            @pl.when(at_end)
+            def _():
+                take(2, so_recv.at[i])
+                for p in range(2):
+                    home(p * half + i)
+
         @pl.when(attends(i))
         def _():
             take(1, so_recv.at[i])
@@ -478,22 +491,26 @@
     def _():
         mixb[2] = jnp.zeros(mixb.shape[1:], mixb.dtype)
 
-    if lent:
-        @pl.when(at_end)
-        def _():
-            for i in range(lent):
-                settle_lent(i)
-
     for i in range(half):
         arrive(i)
-        if i < lent:
+        if bound(i):
             @pl.when(helps)
             def _(i=i):
-                if i == 0:
-                    drain(ql, ql_recv)
-                sol[i, 0], sol[i, 1] = attend([ql[0, i], ql[1, i]], i)
+                j = i - half + lent
+                c = mine(i)
+                if j == 0:
+                    take(4 * lent, ql_recv)
+                sol[j, 0], sol[j, 1] = attend([ql[0, j], ql[1, j]], i)
                 for k in range(2):
-                    sol_copy(i, k, mine(i)).start()
+                    hl[j, k] = add(rl[k, j], sol[j, k])
+
+                def send(to):
+                    for k in range(2):
+                        h_copy(hl.at[j, k], to, 2 * mate + k, i, c).start()
+
+                each_later(send)
+                for k in range(2):
+                    sol_copy(i, k, c).start()
 
             @pl.when(jnp.logical_not(at_end))
             def _(i=i):
@@ -517,7 +534,25 @@
         def _(s=s):
             take(sent_tiles(rows, half, lent, s), sent.at[0])
 
-    take_per_frame(lambda g: (frames - 1 - g) * 2 * chunks, sent.at[1])
+    def take_later(attended):
+        take_per_frame(lambda g: (frames - 1 - g) * (chunks + 2 * attended), sent.at[1])
+
+    if lent:
+        @pl.when(at_end)
+        def _():
+            take_later(half - lent)
+
+        @pl.when(helps)
+        def _():
+            take_later(half + lent)
+
+        if chips > 4:
+            @pl.when(jnp.logical_not(jnp.logical_or(at_end, helps)))
+            def _():
+                take_later(half)
+    else:
+        take_later(half)
+
     for sides in (1, 2):
         @pl.when(edges == sides)
         def _(sides=sides):
@@ -552,7 +587,7 @@
     vmem = pl.BlockSpec(memory_space=pltpu.VMEM)
     outs = (jax.ShapeDtypeStruct(block.shape, bf16),) * 2
     room = max(
-        [sent_tiles(rows, half, lent, s) for s in range(chips)] + [frames * 2 * chunks]
+        [sent_tiles(rows, half, lent, s) for s in range(chips)] + [frames * (2 * chunks + 2 * lent)]
     )
     levels = (frames - 1).bit_length()
     mixed = pl.pallas_call(
@@ -564,6 +599,7 @@
             pltpu.VMEM((rows, half, 2) + tile, bf16),
             pltpu.VMEM((2, half) + tile, bf16),
             pltpu.VMEM((2, held) + tile, bf16),
+            pltpu.VMEM((2, held) + tile, bf16),
             pltpu.VMEM(slab, bf16),
             pltpu.VMEM((half,) + tile, bf16),
             pltpu.VMEM(slab, bf16),
@@ -572,6 +608,7 @@
             pltpu.VMEM((half,) + tile, bf16),
             pltpu.VMEM(slab, bf16),
             pltpu.VMEM((half,) + tile, bf16),
+            pltpu.VMEM((held, 2) + tile, bf16),
             pltpu.VMEM((held, 2) + tile, bf16),
             pltpu.VMEM((frames,) + flat, f32),
             pltpu.VMEM((frames,) + flat, bf16),

time: 24.5 us -> 23.4 us (0.955)
  Pallas kernels: 23.8 us -> 22.6 us
    pallas_call x1, Pallas kernels: 23.1 us -> 21.9 us  [on_device(): pl.pallas_call(functools.partial(block_kernel, frames, rows, chunks, toke...]
where the time goes in v2:
time: 23.4 us; the launch traced here: 23.2 us
  Pallas kernels  22.6 us (97%)
  between operations  0.64 us (3%)
    pallas_call x1, Pallas kernels, on_device(): pl.pallas_call(functools.partial(block_kernel, frames, rows, chunks, toke...  21.9 us
    pallas_call x1, Pallas kernels, on_device(): pl.pallas_call(store_kernel, out_shape=outs, in_specs=[vmem, vmem], out_s...  0.69 us

profile of v2, /device:TPU:21, one launch (start us, length us, event | category | flops | bytes accessed | tf_op | source)
XLA Modules:
  0.0 23.2 jit_solution(738130629202764788)
XLA Ops:
  0.6 21.9 %block.1 = (bf16[1,1,64,768]{3,2,1,0:T(8,128)(2,1)S(1)}, bf16[1,1,64,768]{3,2,1,0:T(8,128)(2,1)S(1)}) custom-call(bf16[1,1,64,768]{3,2,1,0:T(8,128)(2,1)} %res_hbm.1, bf16[1,1,64,768]{3,2,1,0:T(8,128)(2,1)} %q_hbm.1, bf16[1,1,64,768]{3,2,1,0:T(8,128)(2,1)} %k_hbm.1, bf16[1,1,64,768]{3,2,1,0:T(8,128)(2,1)} %v_hbm.1, bf16[1,1,64,768]{3,2,1,0:T(8,128)(2,1)} %qt_hbm.1, ...), custom_call_target="tpu_custom_call" | custom-call | tf_op jit(solution)/shard_map/block/pallas_call | solution.py:593
  22.6 0.7 %store.1 = (bf16[1,1,64,768]{3,2,1,0:T(8,128)(2,1)}, bf16[1,1,64,768]{3,2,1,0:T(8,128)(2,1)}) custom-call(bf16[1,1,64,768]{3,2,1,0:T(8,128)(2,1)S(1)} %get-tuple-element.4.so, bf16[1,1,64,768]{3,2,1,0:T(8,128)(2,1)S(1)} %get-tuple-element.5.bo), custom_call_target="tpu_custom_call" | custom-call | tf_op jit(solution)/shard_map/store/pallas_call | solution.py:628

commit v3 on v2

--- a/solution.py
+++ b/solution.py
@@ -361,7 +361,7 @@
                 send(to)
             return
         ways = [(m, n) for m in range(1, frames) for n in range(m) if m & n == 0]
-        for m, n in sorted(ways, key=lambda way: -bin(way[0] | way[1]).count("1")):
+        for m, n in sorted(ways, key=lambda way: way[0] - way[1]):
             @pl.when(jnp.logical_and(above(m), below(n)) if n else above(m))
             def _(m=m, n=n):
                 send(me_f + m - n)
@@ -524,10 +524,23 @@
 
     drain(cwv, ld.at[3])
     drain(cbv, ld.at[4])
-    for i in range(half):
-        settle(i)
-        weigh(i)
-    for i in range(half):
+    def finish(order):
+        for i in order:
+            settle(i)
+            weigh(i)
+
+    forward = list(range(half))
+    swapped = forward[:-2] + forward[:-3:-1] if lent else forward
+
+    @pl.when(at_end)
+    def _():
+        finish(swapped)
+
+    @pl.when(jnp.logical_not(at_end))
+    def _():
+        finish(forward)
+
+    for i in swapped:
         convolve(i)
     for s in range(chips):
         @pl.when(z == s)

time: 23.4 us -> 23 us (0.983)
  Pallas kernels: 22.6 us -> 22.3 us
    pallas_call x1, Pallas kernels: 21.9 us -> 21.6 us  [on_device(): pl.pallas_call(functools.partial(block_kernel, frames, rows, chunks, toke...]
where the time goes in v3:
time: 23 us; the launch traced here: 22.9 us
  Pallas kernels  22.3 us (97%)
  between operations  0.64 us (3%)
    pallas_call x1, Pallas kernels, on_device(): pl.pallas_call(functools.partial(block_kernel, frames, rows, chunks, toke...  21.6 us
    pallas_call x1, Pallas kernels, on_device(): pl.pallas_call(store_kernel, out_shape=outs, in_specs=[vmem, vmem], out_s...  0.69 us

profile of v3, /device:TPU:21, one launch (start us, length us, event | category | flops | bytes accessed | tf_op | source)
XLA Modules:
  0.0 22.9 jit_solution(7437643007095546018)
XLA Ops:
  0.6 21.6 %block.1 = (bf16[1,1,64,768]{3,2,1,0:T(8,128)(2,1)S(1)}, bf16[1,1,64,768]{3,2,1,0:T(8,128)(2,1)S(1)}) custom-call(bf16[1,1,64,768]{3,2,1,0:T(8,128)(2,1)} %res_hbm.1, bf16[1,1,64,768]{3,2,1,0:T(8,128)(2,1)} %q_hbm.1, bf16[1,1,64,768]{3,2,1,0:T(8,128)(2,1)} %k_hbm.1, bf16[1,1,64,768]{3,2,1,0:T(8,128)(2,1)} %v_hbm.1, bf16[1,1,64,768]{3,2,1,0:T(8,128)(2,1)} %qt_hbm.1, ...), custom_call_target="tpu_custom_call" | custom-call | tf_op jit(solution)/shard_map/block/pallas_call | solution.py:606
  22.2 0.7 %store.1 = (bf16[1,1,64,768]{3,2,1,0:T(8,128)(2,1)}, bf16[1,1,64,768]{3,2,1,0:T(8,128)(2,1)}) custom-call(bf16[1,1,64,768]{3,2,1,0:T(8,128)(2,1)S(1)} %get-tuple-element.4.so, bf16[1,1,64,768]{3,2,1,0:T(8,128)(2,1)S(1)} %get-tuple-element.5.bo), custom_call_target="tpu_custom_call" | custom-call | tf_op jit(solution)/shard_map/store/pallas_call | solution.py:641
